TPU v7x, 32 devices: a whole 2x2x4 slice. The times are simulated.
32 devices in a mesh: tile: 16 (over z, y, x), mode: 2 (over core).
Axes of the slice: x: 2, y: 2, z: 4, core: 2. Of those that a mesh axis runs over, the one named last changes fastest.
Arguments:
- obj: float32 [16, 2, 384, 384], P('tile'), may hold values from -6 to 6
- probe: float32 [4, 2, 256, 256], P('mode'), may hold values from -3 to 3
- mode_weights: float32 [8, 4], P(None, 'mode'), may hold values from 0.25 to 1
- measured: float32 [64, 256, 256], P('tile'), may hold values from 0 to 4
- corner: int32 [64, 2], P('tile'), may hold values from 0 to 383, as said below
- counts: int32 [16], P('tile'), may hold values from 1 to 4, 32 in all
- weight_index: int32 [64], P('tile'), may hold values from 0 to 7
Outputs:
- obj_new: float32 [16, 2, 384, 384], P('tile')
- probe_new: float32 [4, 2, 256, 256], P('mode')
Inputs may be any that keep to these rules, and one draw needn't show every extreme that they name: Tile t has live slots 0 to counts[t] - 1 of its block; the counts sum to 32 and some tile has 4. The first slot of every tile has both corner coordinates between 192 and 320.
All inputs are finite; a program needn't handle non-finite values.
Results may differ from a plain program's by a relative error of at most 0.019.
The roundings to bfloat16 on the way count: a program that leaves them out, or rounds other values in their place, can miss the bound.
Values may be sent and summed in bfloat16 or wider, within the bound.
No kernel may reach another device: no remote copies, remote signals or barrier semaphores. Data moves between devices by JAX's collectives and lax.ppermute only.
A program may use at most 64 MiB of HBM per device.

v0:
```python
import math

import jax
import jax.numpy as jnp
from jax import lax
from jax.sharding import PartitionSpec as P

GC = 8
POS_DEV = 2
ITERS = 2


step_object = 0.1
step_probe = 4.0


def shifted(array, axis, by):
    peers = lax.axis_size(axis)
    return lax.ppermute(array, axis, [(i, (i + by) % peers) for i in range(peers)])


def dft_tables(length, sign):
    index = jnp.arange(length, dtype=jnp.int32)
    product = index[:, None] * index[None, :] % length
    angle = product.astype(jnp.float32) * (2.0 * math.pi / length)
    factor = 1.0 / math.sqrt(length)
    real = jnp.cos(angle) * factor
    imag = sign * jnp.sin(angle) * factor
    left = jnp.concatenate(
        [jnp.concatenate([real, -imag], 1), jnp.concatenate([imag, real], 1)], 0
    ).astype(jnp.bfloat16)
    right = jnp.concatenate([real, imag], 1).astype(jnp.bfloat16)
    return (left, right)


def transform(field, tables):
    left, right = tables
    count = field.shape[0]
    length = field.shape[-1]
    first = jnp.einsum(
        "ij,bjk->bik",
        left,
        field.reshape(count, 2 * length, length),
        preferred_element_type=jnp.float32,
    )
    first = first.astype(jnp.bfloat16).reshape(count, 2, length, length)
    second = jnp.einsum("bcjk,kl->bcjl", first, right, preferred_element_type=jnp.float32)
    real = second[:, 0, :, :length] - second[:, 1, :, length:]
    imag = second[:, 0, :, length:] + second[:, 1, :, :length]
    return jnp.stack([real, imag], 1)


def patch_contributions(
    object_patches, measured, active_mask, mode_weighting, probe, forward_pass, backward_pass, total
):
    count = object_patches.shape[0]
    modes = probe.shape[0]
    length = probe.shape[-1]
    obj_part = object_patches.astype(jnp.float32)[:, None]
    probe_part = probe[None]
    exit_real = probe_part[:, :, 0] * obj_part[:, :, 0] - probe_part[:, :, 1] * obj_part[:, :, 1]
    exit_imag = probe_part[:, :, 0] * obj_part[:, :, 1] + probe_part[:, :, 1] * obj_part[:, :, 0]
    exit_wave = jnp.stack([exit_real, exit_imag], 2).astype(jnp.bfloat16)
    psi = transform(exit_wave.reshape(count * modes, 2, length, length), forward_pass).reshape(
        count, modes, 2, length, length
    )
    power = psi[:, :, 0] * psi[:, :, 0] + psi[:, :, 1] * psi[:, :, 1]
    intensity = total(jnp.sum(mode_weighting[:, :, None, None] * power, 1))
    resid = (intensity - measured) * active_mask[:, None, None]
    scaled = (mode_weighting[:, :, None, None, None] * resid[:, None, None] * psi).astype(
        jnp.bfloat16
    )
    chi = transform(scaled.reshape(count * modes, 2, length, length), backward_pass).reshape(
        count, modes, 2, length, length
    )
    obj_real = jnp.sum(probe_part[:, :, 0] * chi[:, :, 0] + probe_part[:, :, 1] * chi[:, :, 1], 1)
    obj_imag = jnp.sum(probe_part[:, :, 0] * chi[:, :, 1] - probe_part[:, :, 1] * chi[:, :, 0], 1)
    probe_real = jnp.sum(obj_part[:, :, 0] * chi[:, :, 0] + obj_part[:, :, 1] * chi[:, :, 1], 0)
    probe_imag = jnp.sum(obj_part[:, :, 0] * chi[:, :, 1] - obj_part[:, :, 1] * chi[:, :, 0], 0)
    return (jnp.stack([obj_real, obj_imag], 1), jnp.stack([probe_real, probe_imag], 1))


def unchanged(value):
    return value


def body(obj, probe, mode_weights, measured, corner, counts, weight_index):
    patch = probe.shape[-1]
    tile = obj.shape[-1]
    capacity = measured.shape[0]
    kinds = mode_weights.shape[0]
    zero_index = jnp.zeros((), jnp.int32)
    forward_pass = dft_tables(patch, -1.0)
    backward_pass = dft_tables(patch, 1.0)
    active_mask = (jnp.arange(capacity, dtype=jnp.int32) < counts[0]).astype(jnp.float32)
    onehot = (weight_index[:, None] == jnp.arange(kinds, dtype=jnp.int32)[None, :]).astype(
        jnp.float32
    )
    positions = POS_DEV * lax.axis_size("tile")
    state = obj[0]
    probe_now = probe
    for sweep in range(ITERS):
        half = state.astype(jnp.bfloat16)
        right = shifted(half[:, :, :patch], "tile", -1)
        wide = jnp.concatenate([half, right], 2)
        below = shifted(half[:, :patch, :], "tile", -GC)
        diagonal = shifted(half[:, :patch, :patch], "tile", -(GC + 1))
        lower = jnp.concatenate([below, diagonal], 2)
        padded = jnp.concatenate([wide, lower], 1)

        def cut(spot):
            return lax.dynamic_slice(padded, (zero_index, spot[0], spot[1]), (2, patch, patch))

        object_patches = jax.vmap(cut)(corner)
        groups = lax.axis_size("mode")
        mine = lax.axis_index("mode")

        def pick(array):
            shaped = array.reshape((capacity // groups, groups) + array.shape[1:])
            return lax.dynamic_index_in_dim(shaped, mine, 1, keepdims=False)

        all_probe, all_weights = (
            lax.all_gather(probe_now, "mode", axis=0, tiled=True),
            lax.all_gather(mode_weights, "mode", axis=1, tiled=True),
        )
        mode_weighting = jnp.dot(pick(onehot), all_weights, precision=lax.Precision.HIGHEST)
        object_terms, probe_updates = patch_contributions(
            pick(object_patches),
            pick(measured),
            pick(active_mask),
            mode_weighting,
            all_probe,
            forward_pass,
            backward_pass,
            unchanged,
        )
        probe_updates = lax.psum_scatter(
            probe_updates.astype(jnp.bfloat16), "mode", scatter_dimension=0, tiled=True
        ).astype(jnp.float32)
        slot_corner = pick(corner)

        def place(slot, acc):
            spot = slot_corner[slot]
            where = (zero_index, spot[0], spot[1])
            current = lax.dynamic_slice(acc, where, (2, patch, patch))
            return lax.dynamic_update_slice(acc, current + object_terms[slot], where)

        gradient = jnp.zeros((2, tile + patch, tile + patch), jnp.float32)
        gradient = lax.fori_loop(0, object_terms.shape[0], place, gradient)
        above = shifted(gradient[:, tile:, :tile].astype(jnp.bfloat16), "tile", GC).astype(
            jnp.float32
        )
        upper_left = shifted(gradient[:, tile:, tile:].astype(jnp.bfloat16), "tile", GC + 1).astype(
            jnp.float32
        )
        gradient = gradient.at[:, :patch, :tile].add(above)
        gradient = gradient.at[:, :patch, :patch].add(upper_left)
        from_left = shifted(gradient[:, :tile, tile:].astype(jnp.bfloat16), "tile", 1).astype(
            jnp.float32
        )
        tile_grad = gradient[:, :tile, :tile].at[:, :, :patch].add(from_left)
        tile_grad = lax.psum(tile_grad.astype(jnp.bfloat16), "mode").astype(jnp.float32)
        probe_grad = lax.psum(probe_updates, "tile")
        state = state - step_object * tile_grad
        probe_now = probe_now - step_probe / positions * probe_grad
    return (state[None], probe_now)


def solution(mesh):
    placed = (
        P("tile", None, None, None),
        P("mode", None, None, None),
        P(None, "mode"),
        P("tile", None, None),
        P("tile", None),
        P("tile"),
        P("tile"),
    )
    return jax.shard_map(
        body,
        mesh=mesh,
        in_specs=placed,
        out_specs=(P("tile", None, None, None), P("mode", None, None, None)),
        check_vma=False,
    )
```

profile of v0, /device:TPU:0, one launch (start us, length us, event | category | flops | bytes accessed | tf_op | source)
XLA Modules:
  0.0 575.6 jit_solution(13252138141887793834)
XLA Ops:
  8.6 7.0 %collective-permute-start = (bf16[2,384,256]{2,1,0:T(8,128)(2,1)S(1)}, bf16[2,384,256]{2,1,0:T(8,128)(2,1)S(1)}, u32[]{:S(2)}, u32[]{:S(2)}) collective-permute-start(bf16[2,384,256]{2,1,0:T(8,128)(2,1)S(1)} %slice.449), channel_id=1, source_target_pairs={{0,30},{2,0},{4,2},{6,4},{8,6},{10,8},{12,10},{14,12},{16,14},{18,... | collective-permute-start | bytes 1179656 | tf_op jit(solution)/shard_map/ppermute | solution.py:19
  20.2 2.3 all-gather
  25.4 17.5 %collective-permute-done.2 = bf16[2,256,256]{2,1,0:T(8,128)(2,1)S(1)} collective-permute-done((bf16[2,256,256]{2,1,0:T(8,128)(2,1)S(1)}, bf16[2,256,256]{2,1,0:T(8,128)(2,1)S(1)}, u32[]{:S(2)}, u32[]{:S(2)}) %collective-permute-start.2) | collective-permute-done | bytes 262176 | tf_op jit(solution)/shard_map/ppermute | solution.py:19
  42.8 3.6 collective-permute-done.1
  46.6 8.3 %while.36 = (s32[]{:T(128)}, bf16[2,640,640]{2,1,0:T(8,128)(2,1)S(1)}, s32[4,3]{1,0:T(4,128)S(1)}, bf16[4,2,256,256]{3,2,1,0:T(8,128)(2,1)S(1)}, s32[]{:T(128)}) while((s32[]{:T(128)}, bf16[2,640,640]{2,1,0:T(8,128)(2,1)S(1)}, s32[4,3]{1,0:T(4,128)S(1)}, bf16[4,2,256,256]{3,2,1,0:T(8,128)(2,1)S(1)}, s32[]{:T(128)}) %tuple.139), condition=%wide.while_cond.6, body=%wide.while_body.6.sunk | while | flops 2 | bytes 524405 | solution.py:112
  60.8 5.5 subtract_convert_fusion.1
  66.3 4.8 pad_maximum_fusion
  71.1 2.7 convert_element_type.143
  73.8 4.2 convert_bitcast_fusion.3
  78.0 2.8 copy.47
  86.5 4.9 copy.36
  91.4 2.7 convert_element_type.149
  94.1 4.2 convert_bitcast_fusion.2
  98.3 3.0 copy.48
  107.3 24.4 %while.34 = (s32[]{:T(128)}, f32[2,640,640]{2,1,0:T(8,128)}, s32[2,2]{1,0:T(2,128)S(1)}, f32[2,2,256,256]{3,2,1,0:T(8,128)S(1)}, s32[]{:T(128)}, /*index=5*/s32[]{:T(128)}, s32[]{:T(128)}) while((s32[]{:T(128)}, f32[2,640,640]{2,1,0:T(8,128)}, s32[2,2]{1,0:T(2,128)S(1)}, f32[2,2,256,256]{3,2,1,0:T(8,128)S(1)}, s32[]{:T(128)}, ...), condition=%wide.region_4.5_spmd, body=%wide.region_3.4_spmd.sunk | while | flops 131080 | bytes 2621637 | solution.py:149
  113.1 6.6 %dynamic_update_slice.16 = f32[2,640,640]{2,1,0:T(8,128)} dynamic-update-slice(f32[2,640,640]{2,1,0:T(8,128)} %get-tuple-element.475, f32[2,256,256]{2,1,0:T(8,128)S(1)} %bitcast_add_fusion.4, s32[]{:T(128)} %constant.258.clone.1..sunk, s32[]{:T(128)S(6)} %select_n.129, s32[]{:T(128)S(6)} %select_n.130) | dynamic-update-slice | bytes 1048580 | tf_op jit(solution)/shard_map/while/body/eval_jaxpr/dynamic_update_slice | solution.py:146
  125.5 6.1 %dynamic_update_slice.16 = f32[2,640,640]{2,1,0:T(8,128)} dynamic-update-slice(f32[2,640,640]{2,1,0:T(8,128)} %get-tuple-element.475, f32[2,256,256]{2,1,0:T(8,128)S(1)} %bitcast_add_fusion.4, s32[]{:T(128)} %constant.258.clone.1..sunk, s32[]{:T(128)S(6)} %select_n.129, s32[]{:T(128)S(6)} %select_n.130) | dynamic-update-slice | bytes 1048580 | tf_op jit(solution)/shard_map/while/body/eval_jaxpr/dynamic_update_slice | solution.py:146
  131.7 2.2 convert.89
  135.5 24.9 %collective-permute-done.3 = bf16[2,256,384]{2,1,0:T(8,128)(2,1)S(1)} collective-permute-done((bf16[2,256,384]{2,1,0:T(8,128)(2,1)S(1)}, bf16[2,256,384]{2,1,0:T(8,128)(2,1)S(1)}, u32[]{:S(2)}, u32[]{:S(2)}) %collective-permute-start.3) | collective-permute-done | bytes 393248 | tf_op jit(solution)/shard_map/ppermute | solution.py:19
  160.8 5.8 %collective-permute-start.5 = (bf16[2,384,256]{2,1,0:T(8,128)(2,1)S(1)}, bf16[2,384,256]{2,1,0:T(8,128)(2,1)S(1)}, u32[]{:S(2)}, u32[]{:S(2)}) collective-permute-start(bf16[2,384,256]{2,1,0:T(8,128)(2,1)S(1)} %slice.531), channel_id=1, source_target_pairs={{0,2},{2,4},{4,6},{6,8},{8,10},{10,12},{12,14},{14,16},{16,18},{18... | collective-permute-start | bytes 1179656 | tf_op jit(solution)/shard_map/ppermute | solution.py:19
  166.7 7.6 %collective-permute-done.5 = bf16[2,384,256]{2,1,0:T(8,128)(2,1)S(1)} collective-permute-done((bf16[2,384,256]{2,1,0:T(8,128)(2,1)S(1)}, bf16[2,384,256]{2,1,0:T(8,128)(2,1)S(1)}, u32[]{:S(2)}, u32[]{:S(2)}) %collective-permute-start.5) | collective-permute-done | bytes 393248 | tf_op jit(solution)/shard_map/ppermute | solution.py:19
  176.4 17.5 %all-reduce.5.cloned.1.call-done = bf16[2,384,384]{2,1,0:T(8,128)(2,1)} async-done(((bf16[2,384,384]{2,1,0:T(8,128)(2,1)}), bf16[2,384,384]{2,1,0:T(8,128)(2,1)}) %all-reduce.5.cloned.1.call-update) | async-done | bytes 589840 | tf_op jit(solution)/shard_map/psum | solution.py:162
  197.4 5.4 collective-permute-start.6
  204.0 2.3 reduce-scatter.3.cloned.1.call-done
  206.3 103.1 %all-reduce.8 = f32[2,2,256,256]{3,2,1,0:T(8,128)} all-reduce(bf16[2,2,256,256]{3,2,1,0:T(8,128)(2,1)} %reduce-scatter.3.cloned.1.call-done), channel_id=1, replica_groups=mesh['tile'=16,'mode'=2] {'tile'}, use_global_device_ids=true, to_apply=%region_9.10 | all-reduce | flops 262144 | bytes 1572864 | tf_op jit(solution)/shard_map/psum | solution.py:163
  309.4 2.4 multiply_subtract_fusion.1
  315.0 11.4 %while.37 = (s32[]{:T(128)}, bf16[2,640,640]{2,1,0:T(8,128)(2,1)S(1)}, s32[4,3]{1,0:T(4,128)S(1)}, bf16[4,2,256,256]{3,2,1,0:T(8,128)(2,1)}, s32[]{:T(128)}) while((s32[]{:T(128)}, bf16[2,640,640]{2,1,0:T(8,128)(2,1)S(1)}, s32[4,3]{1,0:T(4,128)S(1)}, bf16[4,2,256,256]{3,2,1,0:T(8,128)(2,1)}, s32[]{:T(128)}) %tuple.163), condition=%wide.while_cond.7, body=%wide.while_body.7.sunk | while | flops 2 | bytes 525929 | solution.py:112
  334.6 5.7 subtract_convert_fusion
  340.2 4.8 pad_maximum_fusion.1
  345.1 2.7 convert_element_type.160
  347.7 4.2 convert_bitcast_fusion.1
  351.9 2.8 copy.49
  360.5 4.9 copy.43
  365.4 2.7 convert_element_type.164
  368.0 4.2 convert_bitcast_fusion
  372.2 3.1 copy.50
  378.4 2.2 fusion.7
  382.6 24.3 %while.35 = (s32[]{:T(128)}, f32[2,640,640]{2,1,0:T(8,128)}, s32[2,2]{1,0:T(2,128)S(1)}, f32[2,2,256,256]{3,2,1,0:T(8,128)S(1)}, s32[]{:T(128)}, /*index=5*/s32[]{:T(128)}, s32[]{:T(128)}) while((s32[]{:T(128)}, f32[2,640,640]{2,1,0:T(8,128)}, s32[2,2]{1,0:T(2,128)S(1)}, f32[2,2,256,256]{3,2,1,0:T(8,128)S(1)}, s32[]{:T(128)}, ...), condition=%wide.region_14.15_spmd, body=%wide.region_13.14_spmd.sunk | while | flops 131080 | bytes 2621637 | solution.py:149
  388.4 6.6 %dynamic_update_slice.17 = f32[2,640,640]{2,1,0:T(8,128)} dynamic-update-slice(f32[2,640,640]{2,1,0:T(8,128)} %get-tuple-element.511, f32[2,256,256]{2,1,0:T(8,128)S(1)} %bitcast_add_fusion.5, s32[]{:T(128)} %constant.258.clone.1..sunk.1, s32[]{:T(128)S(6)} %select_n.131, s32[]{:T(128)S(6)} %select_n.132) | dynamic-update-slice | bytes 1048580 | tf_op jit(solution)/shard_map/while/body/eval_jaxpr/dynamic_update_slice | solution.py:146
  400.8 6.1 %dynamic_update_slice.17 = f32[2,640,640]{2,1,0:T(8,128)} dynamic-update-slice(f32[2,640,640]{2,1,0:T(8,128)} %get-tuple-element.511, f32[2,256,256]{2,1,0:T(8,128)S(1)} %bitcast_add_fusion.5, s32[]{:T(128)} %constant.258.clone.1..sunk.1, s32[]{:T(128)S(6)} %select_n.131, s32[]{:T(128)S(6)} %select_n.132) | dynamic-update-slice | bytes 1048580 | tf_op jit(solution)/shard_map/while/body/eval_jaxpr/dynamic_update_slice | solution.py:146
  406.9 2.2 convert.95
  410.1 17.2 %collective-permute-done.9 = bf16[2,256,384]{2,1,0:T(8,128)(2,1)S(1)} collective-permute-done((bf16[2,256,384]{2,1,0:T(8,128)(2,1)S(1)}, bf16[2,256,384]{2,1,0:T(8,128)(2,1)S(1)}, u32[]{:S(2)}, u32[]{:S(2)}) %collective-permute-start.9) | collective-permute-done | bytes 393248 | tf_op jit(solution)/shard_map/ppermute | solution.py:19
  427.8 6.0 %collective-permute-start.11 = (bf16[2,384,256]{2,1,0:T(8,128)(2,1)S(1)}, bf16[2,384,256]{2,1,0:T(8,128)(2,1)S(1)}, u32[]{:S(2)}, u32[]{:S(2)}) collective-permute-start(bf16[2,384,256]{2,1,0:T(8,128)(2,1)S(1)} %slice.530), channel_id=1, source_target_pairs={{0,2},{2,4},{4,6},{6,8},{8,10},{10,12},{12,14},{14,16},{16,18},{18... | collective-permute-start | bytes 1179656 | tf_op jit(solution)/shard_map/ppermute | solution.py:19
  433.8 12.8 %collective-permute-done.11 = bf16[2,384,256]{2,1,0:T(8,128)(2,1)S(1)} collective-permute-done((bf16[2,384,256]{2,1,0:T(8,128)(2,1)S(1)}, bf16[2,384,256]{2,1,0:T(8,128)(2,1)S(1)}, u32[]{:S(2)}, u32[]{:S(2)}) %collective-permute-start.11) | collective-permute-done | bytes 393248 | tf_op jit(solution)/shard_map/ppermute | solution.py:19
  448.7 15.3 %all-reduce.7.cloned.1.call-done = bf16[2,384,384]{2,1,0:T(8,128)(2,1)} async-done(((bf16[2,384,384]{2,1,0:T(8,128)(2,1)}), bf16[2,384,384]{2,1,0:T(8,128)(2,1)}) %all-reduce.7.cloned.1.call-update) | async-done | bytes 589840 | tf_op jit(solution)/shard_map/psum | solution.py:162
  464.0 2.3 subtract_bitcast_fusion
  466.3 10.0 %reduce-scatter.5.cloned.1.call-done = bf16[2,2,256,256]{3,2,1,0:T(8,128)(2,1)} async-done(((bf16[4,2,256,256]{3,2,1,0:T(8,128)(2,1)}), bf16[2,2,256,256]{3,2,1,0:T(8,128)(2,1)}) %reduce-scatter.5.cloned.1.call-update) | async-done | bytes 524304 | tf_op jit(solution)/shard_map/reduce_scatter | solution.py:137
  476.3 91.1 %all-reduce.9 = f32[2,2,256,256]{3,2,1,0:T(8,128)S(1)} all-reduce(bf16[2,2,256,256]{3,2,1,0:T(8,128)(2,1)} %reduce-scatter.5.cloned.1.call-done), channel_id=1, replica_groups=mesh['tile'=16,'mode'=2] {'tile'}, use_global_device_ids=true, to_apply=%region_19.20 | all-reduce | flops 262144 | bytes 1572864 | tf_op jit(solution)/shard_map/psum | solution.py:163
  (218 shorter events, 88.1 us)
Async XLA Ops:
  7.2 50.2 %all-gather.4.cloned.1.call-start = ((), (), s32[]{:S(2)}) async-start(), calls=%async_computation.2 | async-start | bytes 3145728 | tf_op jit(solution)/shard_map/all_gather | solution.py:123
  8.5 11.2 %copy-start.33 = (s32[4,2]{0,1:T(2,128)S(1)}, s32[4,2]{0,1:T(2,128)}, u32[]{:S(2)}) copy-start(s32[4,2]{0,1:T(2,128)} %param.27) | copy-start | bytes 100
  8.6 11.4 %copy-start.35 = (s32[4]{0:T(128)S(1)}, s32[4]{0:T(128)}, u32[]{:S(2)}) copy-start(s32[4]{0:T(128)} %param.29) | copy-start | bytes 52
  8.6 11.6 %copy-start.34 = (f32[8,2]{0,1:T(2,128)S(1)}, f32[8,2]{0,1:T(2,128)}, u32[]{:S(2)}) copy-start(f32[8,2]{0,1:T(2,128)} %param.25) | copy-start | bytes 196
  8.6 34.2 %collective-permute-start = (bf16[2,384,256]{2,1,0:T(8,128)(2,1)S(1)}, bf16[2,384,256]{2,1,0:T(8,128)(2,1)S(1)}, u32[]{:S(2)}, u32[]{:S(2)}) collective-permute-start(bf16[2,384,256]{2,1,0:T(8,128)(2,1)S(1)} %slice.449), channel_id=1, source_target_pairs={{0,30},{2,0},{4,2},{6,4},{8,6},{10,8},{12,10},{14,12},{16,14},{18,... | collective-permute-start | bytes 1179656 | tf_op jit(solution)/shard_map/ppermute | solution.py:19
  15.7 30.7 %collective-permute-start.1 = (bf16[2,256,384]{2,1,0:T(8,128)(2,1)S(1)}, bf16[2,256,384]{2,1,0:T(8,128)(2,1)S(1)}, u32[]{:S(2)}, u32[]{:S(2)}) collective-permute-start(bf16[2,256,384]{2,1,0:T(8,128)(2,1)S(1)} %slice.450), channel_id=1, source_target_pairs={{0,16},{2,18},{4,20},{6,22},{8,24},{10,26},{12,28},{14,30},{16,0},... | collective-permute-start | bytes 1179656 | tf_op jit(solution)/shard_map/ppermute | solution.py:19
  15.8 27.0 %collective-permute-start.2 = (bf16[2,256,256]{2,1,0:T(8,128)(2,1)S(1)}, bf16[2,256,256]{2,1,0:T(8,128)(2,1)S(1)}, u32[]{:S(2)}, u32[]{:S(2)}) collective-permute-start(bf16[2,256,256]{2,1,0:T(8,128)(2,1)S(1)} %slice.451), channel_id=1, source_target_pairs={{0,14},{2,16},{4,18},{6,20},{8,22},{10,24},{12,26},{14,28},{16,30}... | collective-permute-start | bytes 786440 | tf_op jit(solution)/shard_map/ppermute | solution.py:19
  16.9 176.9 %all-reduce.5.cloned.1.call-start = ((), (), s32[]{:S(2)}) async-start(), calls=%async_computation.3 | async-start | bytes 1179648 | tf_op jit(solution)/shard_map/psum | solution.py:162
  19.7 61.1 %copy-start.24 = (bf16[256,256]{1,0:T(8,128)(2,1)}, bf16[256,256]{1,0:T(8,128)(2,1)S(1)}, u32[]{:S(2)}) copy-start(bf16[256,256]{1,0:T(8,128)(2,1)S(1)} %multiply_convert_fusion.2) | copy-start | bytes 393220
  55.1 2.2 copy-start.14
  55.1 2.2 copy-start.16
  59.1 1.7 copy-start.8
  71.1 2.7 copy-start.31
  83.0 1.2 copy-start.28
  91.4 2.7 copy-start.26
  91.4 2.7 copy-start.32
  102.6 1.3 copy-start.15
  102.6 1.5 copy-start.17
  131.7 28.7 %copy-start.1 = (f32[2,640,640]{2,1,0:T(8,128)S(1)}, f32[2,640,640]{2,1,0:T(8,128)}, u32[]{:S(2)}) copy-start(f32[2,640,640]{2,1,0:T(8,128)} %get-tuple-element.232) | copy-start | bytes 9830404
  134.0 26.4 %collective-permute-start.3 = (bf16[2,256,384]{2,1,0:T(8,128)(2,1)S(1)}, bf16[2,256,384]{2,1,0:T(8,128)(2,1)S(1)}, u32[]{:S(2)}, u32[]{:S(2)}) collective-permute-start(bf16[2,256,384]{2,1,0:T(8,128)(2,1)S(1)} %slice.463), channel_id=1, source_target_pairs={{0,16},{2,18},{4,20},{6,22},{8,24},{10,26},{12,28},{14,30},{16,0},... | collective-permute-start | bytes 1179656 | tf_op jit(solution)/shard_map/ppermute | solution.py:19
  134.2 26.4 %collective-permute-start.4 = (bf16[2,256,256]{2,1,0:T(8,128)(2,1)S(1)}, bf16[2,256,256]{2,1,0:T(8,128)(2,1)S(1)}, u32[]{:S(2)}, u32[]{:S(2)}) collective-permute-start(bf16[2,256,256]{2,1,0:T(8,128)(2,1)S(1)} %slice.465), channel_id=1, source_target_pairs={{0,18},{2,20},{4,22},{6,24},{8,26},{10,28},{12,30},{14,0},{16,2},{... | collective-permute-start | bytes 786440 | tf_op jit(solution)/shard_map/ppermute | solution.py:19
  160.8 13.5 %collective-permute-start.5 = (bf16[2,384,256]{2,1,0:T(8,128)(2,1)S(1)}, bf16[2,384,256]{2,1,0:T(8,128)(2,1)S(1)}, u32[]{:S(2)}, u32[]{:S(2)}) collective-permute-start(bf16[2,384,256]{2,1,0:T(8,128)(2,1)S(1)} %slice.531), channel_id=1, source_target_pairs={{0,2},{2,4},{4,6},{6,8},{8,10},{10,12},{12,14},{14,16},{16,18},{18... | collective-permute-start | bytes 1179656 | tf_op jit(solution)/shard_map/ppermute | solution.py:19
  174.4 19.5 %copy-start.2 = (f32[1,2,384,384]{3,2,1,0:T(8,128)S(1)}, f32[1,2,384,384]{3,2,1,0:T(8,128)}, u32[]{:S(2)}) copy-start(f32[1,2,384,384]{3,2,1,0:T(8,128)} %param.23) | copy-start | bytes 3538948
  175.2 31.1 %reduce-scatter.3.cloned.1.call-start = ((), (), s32[]{:S(2)}) async-start(), calls=%async_computation.4 | async-start | bytes 1572864 | tf_op jit(solution)/shard_map/reduce_scatter | solution.py:137
  176.3 153.5 %all-gather.6.cloned.1.call-start = ((), (), s32[]{:S(2)}) async-start(), calls=%async_computation.5 | async-start | bytes 3145728 | tf_op jit(solution)/shard_map/all_gather | solution.py:123
  195.1 114.3 %copy-start.18 = (f32[2,2,256,256]{3,2,1,0:T(8,128)S(1)}, f32[2,2,256,256]{3,2,1,0:T(8,128)}, u32[]{:S(2)}) copy-start(f32[2,2,256,256]{3,2,1,0:T(8,128)} %param.24) | copy-start | bytes 3145732
  197.4 114.4 %collective-permute-start.6 = (bf16[2,384,256]{2,1,0:T(8,128)(2,1)}, bf16[2,384,256]{2,1,0:T(8,128)(2,1)S(1)}, u32[]{:S(2)}, u32[]{:S(2)}) collective-permute-start(bf16[2,384,256]{2,1,0:T(8,128)(2,1)} %slice.470), channel_id=1, source_target_pairs={{0,30},{2,0},{4,2},{6,4},{8,6},{10,8},{12,10},{14,12},{16,14},{18,... | collective-permute-start | bytes 1179656 | tf_op jit(solution)/shard_map/ppermute | solution.py:19
  202.9 109.8 %collective-permute-start.7 = (bf16[2,256,384]{2,1,0:T(8,128)(2,1)}, bf16[2,256,384]{2,1,0:T(8,128)(2,1)}, u32[]{:S(2)}, u32[]{:S(2)}) collective-permute-start(bf16[2,256,384]{2,1,0:T(8,128)(2,1)} %slice.471), channel_id=1, source_target_pairs={{0,16},{2,18},{4,20},{6,22},{8,24},{10,26},{12,28},{14,30},{16,0},... | collective-permute-start | bytes 1179656 | tf_op jit(solution)/shard_map/ppermute | solution.py:19
  202.9 109.0 %collective-permute-start.8 = (bf16[2,256,256]{2,1,0:T(8,128)(2,1)}, bf16[2,256,256]{2,1,0:T(8,128)(2,1)}, u32[]{:S(2)}, u32[]{:S(2)}) collective-permute-start(bf16[2,256,256]{2,1,0:T(8,128)(2,1)} %slice.472), channel_id=1, source_target_pairs={{0,14},{2,16},{4,18},{6,20},{8,22},{10,24},{12,26},{14,28},{16,30}... | collective-permute-start | bytes 786440 | tf_op jit(solution)/shard_map/ppermute | solution.py:19
  311.8 152.2 %all-reduce.7.cloned.1.call-start = ((), (), s32[]{:S(2)}) async-start(), calls=%async_computation.6 | async-start | bytes 1179648 | tf_op jit(solution)/shard_map/psum | solution.py:162
  327.6 2.2 copy-start.10
  327.6 2.2 copy-start.12
  331.6 3.0 copy-start.4
  331.6 3.0 copy-start.6
  345.1 2.7 copy-start.25
  365.4 2.7 copy-start.27
  376.6 1.5 copy-start.7
  376.6 1.7 copy-start.11
  376.6 1.8 copy-start.13
  406.9 20.4 %copy-start = (f32[2,640,640]{2,1,0:T(8,128)S(1)}, f32[2,640,640]{2,1,0:T(8,128)}, u32[]{:S(2)}) copy-start(f32[2,640,640]{2,1,0:T(8,128)} %get-tuple-element.233) | copy-start | bytes 9830404
  409.2 18.1 %collective-permute-start.9 = (bf16[2,256,384]{2,1,0:T(8,128)(2,1)S(1)}, bf16[2,256,384]{2,1,0:T(8,128)(2,1)S(1)}, u32[]{:S(2)}, u32[]{:S(2)}) collective-permute-start(bf16[2,256,384]{2,1,0:T(8,128)(2,1)S(1)} %slice.484), channel_id=1, source_target_pairs={{0,16},{2,18},{4,20},{6,22},{8,24},{10,26},{12,28},{14,30},{16,0},... | collective-permute-start | bytes 1179656 | tf_op jit(solution)/shard_map/ppermute | solution.py:19
  409.3 18.3 %collective-permute-start.10 = (bf16[2,256,256]{2,1,0:T(8,128)(2,1)S(1)}, bf16[2,256,256]{2,1,0:T(8,128)(2,1)S(1)}, u32[]{:S(2)}, u32[]{:S(2)}) collective-permute-start(bf16[2,256,256]{2,1,0:T(8,128)(2,1)S(1)} %slice.486), channel_id=1, source_target_pairs={{0,18},{2,20},{4,22},{6,24},{8,26},{10,28},{12,30},{14,0},{16,2},{... | collective-permute-start | bytes 786440 | tf_op jit(solution)/shard_map/ppermute | solution.py:19
  427.7 19.9 %copy-start.22 = (bf16[4,256,256]{2,1,0:T(8,128)(2,1)S(1)}, bf16[4,256,256]{2,1,0:T(8,128)(2,1)}, u32[]{:S(2)}) copy-start(bf16[4,256,256]{2,1,0:T(8,128)(2,1)} %get-tuple-element.254) | copy-start | bytes 1572868
  427.7 19.9 %copy-start.23 = (bf16[4,256,256]{2,1,0:T(8,128)(2,1)S(1)}, bf16[4,256,256]{2,1,0:T(8,128)(2,1)}, u32[]{:S(2)}) copy-start(bf16[4,256,256]{2,1,0:T(8,128)(2,1)} %get-tuple-element.255) | copy-start | bytes 1572868
  427.8 18.8 %collective-permute-start.11 = (bf16[2,384,256]{2,1,0:T(8,128)(2,1)S(1)}, bf16[2,384,256]{2,1,0:T(8,128)(2,1)S(1)}, u32[]{:S(2)}, u32[]{:S(2)}) collective-permute-start(bf16[2,384,256]{2,1,0:T(8,128)(2,1)S(1)} %slice.530), channel_id=1, source_target_pairs={{0,2},{2,4},{4,6},{6,8},{8,10},{10,12},{12,14},{14,16},{16,18},{18... | collective-permute-start | bytes 1179656 | tf_op jit(solution)/shard_map/ppermute | solution.py:19
  446.7 17.3 %copy-start.19 = (bf16[2,384,384]{2,1,0:T(8,128)(2,1)S(1)}, bf16[2,384,384]{2,1,0:T(8,128)(2,1)}, u32[]{:S(2)}) copy-start(bf16[2,384,384]{2,1,0:T(8,128)(2,1)} %all-reduce.5.cloned.1.call-done) | copy-start | bytes 1769476
  447.5 28.8 %reduce-scatter.5.cloned.1.call-start = ((), (), s32[]{:S(2)}) async-start(), calls=%async_computation.7 | async-start | bytes 1572864 | tf_op jit(solution)/shard_map/reduce_scatter | solution.py:137
  448.7 118.7 %copy-start.3 = (f32[2,2,256,256]{3,2,1,0:T(8,128)S(1)}, f32[2,2,256,256]{3,2,1,0:T(8,128)}, u32[]{:S(2)}) copy-start(f32[2,2,256,256]{3,2,1,0:T(8,128)} %multiply_subtract_fusion.1) | copy-start | bytes 3145732
  (6 other events, 6.1 us)
Sparse Core Ops, SparseCore 0:
  17.1 9.6 all-gather.3
  175.3 18.5 all-reduce.4
  196.7 9.5 reduce-scatter.2
  311.9 7.9 all-gather.5
  447.6 16.2 all-reduce.6
  466.6 9.5 reduce-scatter.4
where the time goes:
time: 581 us; the launch traced here: 576 us
  blocking collectives  196 us (34%)
  waiting for transfers between devices  129 us (22%)
  local copies, waits for them, and re-layouts  107 us (18%)
  other arithmetic  61 us (10%)
  starting transfers between devices  29.3 us (5%)
  matrix products  22 us (4%)
  between operations  15.9 us (3%)
  loops' own time  15.8 us (3%)
    psum x2, blocking collectives, body(): probe_grad = lax.psum(probe_updates, 'tile')  194 us
    ppermute x12, waiting for transfers between devices, shifted(): lax.ppermute(array, axis, [(i, (i + by) % peers) for i in range(peers)])  83.4 us
    psum x2, waiting for transfers between devices, body(): lax.psum(tile_grad.astype(jnp.bfloat16), 'mode').astype(jnp.float32)  32.8 us
    ppermute x12, starting transfers between devices, shifted(): lax.ppermute(array, axis, [(i, (i + by) % peers) for i in range(peers)])  29 us
    dynamic_update_slice x4, local copies, waits for them, and re-layouts, place(): return lax.dynamic_update_slice(acc, current + object_terms[slot], where)  25.4 us
    another operation x7, other arithmetic  20.1 us
    gather x24, local copies, waits for them, and re-layouts  19.3 us
    dot_general x4, matrix products, transform(): jnp.einsum('ij,bjk->bik', left, field.reshape(count, 2 * length, length),...  16.8 us
  transfers between devices with their start and end apart: 18, of which 10 were waited for; matrix products, arithmetic and copies ran while one was open for 8% of the time, Pallas kernels for 0%

commit v1 on v0

v1 whole, which is shorter than its diff:
```python
import functools
import math

import jax
import jax.numpy as jnp
from jax import lax
from jax.experimental import pallas as pl
from jax.experimental.pallas import tpu as pltpu
from jax.sharding import PartitionSpec as P

GC = 8
POS_DEV = 2
ITERS = 2
STRIP = 32

step_object = 0.1
step_probe = 4.0

f32 = jnp.float32
bf16 = jnp.bfloat16
VM = pl.BlockSpec(memory_space=pltpu.VMEM)
SM = pl.BlockSpec(memory_space=pltpu.SMEM)


def shifted(array, by):
    peers = lax.axis_size("tile")
    return lax.ppermute(array, "tile", [(i, (i + by) % peers) for i in range(peers)])


def flipped(array, mask):
    peers = lax.axis_size("tile")
    return lax.ppermute(array, "tile", [(i, i ^ mask) for i in range(peers)])


def swapped(array):
    return lax.ppermute(array, "mode", [(0, 1), (1, 0)])


def dft_tables(length):
    index = jnp.arange(length, dtype=jnp.int32)
    product = index[:, None] * index[None, :] % length
    angle = product.astype(f32) * (2.0 * math.pi / length)
    factor = 1.0 / math.sqrt(length)
    real = jnp.cos(angle) * factor
    imag = -(jnp.sin(angle) * factor)
    one = jnp.concatenate(
        [jnp.concatenate([real, -imag], 1), jnp.concatenate([imag, real], 1)], 0
    ).astype(bf16)
    two = jnp.concatenate(
        [jnp.concatenate([real, imag], 1), jnp.concatenate([-imag, real], 1)], 0
    ).astype(bf16)
    return one, two


def dot(a, b):
    return jnp.dot(a, b, preferred_element_type=f32)


def patch_kernel(
    info, corner, kind, wm, wo,
    tm, rm, bm, dm, to, ro, bo, do, meas, pm, po, one, two,
    keep, send, pgm, pgo,
    frame, grad, psi, xs, ts, orr, oii, term, acc,
):
    n = pm.shape[-1]
    t = tm.shape[-1]
    half = pm.shape[0]
    modes = 2 * half
    me = info[0]
    live = info[1]
    for plane, (a, b, c, d) in ((me, (tm, rm, bm, dm)), (1 - me, (to, ro, bo, do))):
        frame[plane, pl.ds(0, t), pl.ds(0, t)] = a[...].astype(f32)
        frame[plane, pl.ds(0, t), pl.ds(t, n)] = b[...].astype(f32)
        frame[plane, pl.ds(t, n), pl.ds(0, t)] = c[...].astype(f32)
        frame[plane, pl.ds(t, n), pl.ds(t, n)] = d[...].astype(f32)
    grad[...] = jnp.zeros_like(grad)
    acc[...] = jnp.zeros_like(acc)

    def probe_at(m, c, rows):
        ref = pm if m < half else po
        return ref[m % half, c, rows, :]

    def slot_body(g, carry):
        s = me + 2 * g

        @pl.when(s < live)
        def _():
            row = corner[s, 0]
            col = corner[s, 1]
            rb = pl.multiple_of(row // 8 * 8, 8)
            rr = row - rb
            cb = pl.multiple_of(col // 128 * 128, 128)
            cc = col - cb
            high, wide = n + 8, n + 128
            for p, out in ((0, orr), (1, oii)):
                win = frame[p, pl.ds(rb, high), pl.ds(cb, wide)]
                win = pltpu.roll(win, lax.rem(wide - cc, wide), 1)[:, :n]
                win = pltpu.roll(win, lax.rem(high - rr, high), 0)[:n]
                out[...] = win
            strips = [pl.ds(i * STRIP, STRIP) for i in range(n // STRIP)]
            lower = [pl.ds(n + i * STRIP, STRIP) for i in range(n // STRIP)]
            w = [wm[kind[s], m] if m < half else wo[kind[s], m - half] for m in range(modes)]
            for m in range(modes):
                for up, lo in zip(strips, lower):
                    a, b = orr[up, :], oii[up, :]
                    pr, pi = probe_at(m, 0, up), probe_at(m, 1, up)
                    xs[m, up, :] = (pr * a - pi * b).astype(bf16)
                    xs[m, lo, :] = (pr * b + pi * a).astype(bf16)
            for m in range(modes):
                y = dot(one[...], xs[m])
                ts[pl.ds(m * n, n), pl.ds(0, n)] = y[:n].astype(bf16)
                ts[pl.ds(m * n, n), pl.ds(n, n)] = y[n:].astype(bf16)
            psi[...] = dot(ts[...], two[...])
            for i, (up, lo) in enumerate(zip(strips, lower)):
                total = jnp.zeros((STRIP, n), f32)
                for m in range(modes):
                    rows = pl.ds(m * n + i * STRIP, STRIP)
                    a, b = psi[rows, pl.ds(0, n)], psi[rows, pl.ds(n, n)]
                    total = total + w[m] * (a * a + b * b)
                resid = total - meas[s, up, :]
                for m in range(modes):
                    rows = pl.ds(m * n + i * STRIP, STRIP)
                    scale = w[m] * resid
                    xs[m, up, :] = (scale * psi[rows, pl.ds(0, n)]).astype(bf16)
                    xs[m, lo, :] = (scale * psi[rows, pl.ds(n, n)]).astype(bf16)
            for m in range(modes):
                y = dot(two[...], xs[m])
                ts[pl.ds(m * n, n), pl.ds(0, n)] = y[:n].astype(bf16)
                ts[pl.ds(m * n, n), pl.ds(n, n)] = y[n:].astype(bf16)
            psi[...] = dot(ts[...], one[...])
            for i, up in enumerate(strips):
                a, b = orr[up, :], oii[up, :]
                tr = jnp.zeros((STRIP, n), f32)
                ti = jnp.zeros((STRIP, n), f32)
                for m in range(modes):
                    rows = pl.ds(m * n + i * STRIP, STRIP)
                    cr, ci = psi[rows, pl.ds(0, n)], psi[rows, pl.ds(n, n)]
                    pr, pi = probe_at(m, 0, up), probe_at(m, 1, up)
                    tr = tr + (pr * cr + pi * ci)
                    ti = ti + (pr * ci - pi * cr)
                    acc[m, 0, up, :] += a * cr + b * ci
                    acc[m, 1, up, :] += a * ci - b * cr
                term[0, up, pl.ds(0, n)] = tr
                term[1, up, pl.ds(0, n)] = ti
            for p in range(2):
                term[p, pl.ds(n, 8), :] = jnp.zeros((8, wide), f32)
                term[p, pl.ds(0, n), pl.ds(n, 128)] = jnp.zeros((n, 128), f32)
                moved = pltpu.roll(pltpu.roll(term[p], rr, 0), cc, 1)
                grad[p, pl.ds(rb, high), pl.ds(cb, wide)] += moved

        return carry

    lax.fori_loop(0, meas.shape[0] // 2, slot_body, 0)
    keep[...] = grad[me]
    send[...] = grad[1 - me].astype(bf16)
    for m in range(half):
        pgm[m] = acc[m]
        pgo[m] = acc[half + m].astype(bf16)


def patches(info, corner, kind, wm, wo, mine, other, meas, pm, po, one, two):
    n = pm.shape[-1]
    t = mine[0].shape[-1]
    f = n + t
    modes = 2 * pm.shape[0]
    return pl.pallas_call(
        patch_kernel,
        out_shape=(
            jax.ShapeDtypeStruct((f, f), f32),
            jax.ShapeDtypeStruct((f, f), bf16),
            jax.ShapeDtypeStruct(pm.shape, f32),
            jax.ShapeDtypeStruct(pm.shape, bf16),
        ),
        in_specs=[SM] * 5 + [VM] * 13,
        out_specs=(VM,) * 4,
        scratch_shapes=[
            pltpu.VMEM((2, f, f), f32),
            pltpu.VMEM((2, f, f), f32),
            pltpu.VMEM((modes * n, 2 * n), f32),
            pltpu.VMEM((modes, 2 * n, n), bf16),
            pltpu.VMEM((modes * n, 2 * n), bf16),
            pltpu.VMEM((n, n), f32),
            pltpu.VMEM((n, n), f32),
            pltpu.VMEM((2, n + 8, n + 128), f32),
            pltpu.VMEM((modes, 2, n, n), f32),
        ],
        compiler_params=pltpu.CompilerParams(vmem_limit_bytes=60 * 1024 * 1024),
        name="patch",
    )(info, corner, kind, wm, wo, *mine, *other, meas, pm, po, one, two)


def margin_kernel(keep, got, own, right, low, diag):
    t = own.shape[0]
    f = keep.shape[0]
    n = f - t
    own[...] = keep[:t, :t] + got[:t, :t].astype(f32)
    right[...] = (keep[:t, t:] + got[:t, t:].astype(f32)).astype(bf16)
    low[...] = (keep[t:, :t] + got[t:, :t].astype(f32)).astype(bf16)
    diag[...] = (keep[t:, t:] + got[t:, t:].astype(f32)).astype(bf16)


def margins(keep, got, t):
    n = keep.shape[0] - t
    return pl.pallas_call(
        margin_kernel,
        out_shape=(
            jax.ShapeDtypeStruct((t, t), f32),
            jax.ShapeDtypeStruct((t, n), bf16),
            jax.ShapeDtypeStruct((n, t), bf16),
            jax.ShapeDtypeStruct((n, n), bf16),
        ),
        in_specs=[VM] * 2,
        out_specs=(VM,) * 4,
        name="margin",
    )(keep, got)


def update_kernel(state, own, right, low, diag, new, half, hr, hl, hd):
    n = diag.shape[0]
    new[...] = own[...]
    new[:, :n] += right[...].astype(f32)
    new[:n, :] += low[...].astype(f32)
    new[:n, :n] += diag[...].astype(f32)
    value = state[...] - step_object * new[...]
    new[...] = value
    small = value.astype(bf16)
    half[...] = small
    hr[...] = small[:, :n]
    hl[...] = small[:n, :]
    hd[...] = small[:n, :n]


def update(state, own, right, low, diag):
    t = state.shape[0]
    n = diag.shape[0]
    return pl.pallas_call(
        update_kernel,
        out_shape=(
            jax.ShapeDtypeStruct((t, t), f32),
            jax.ShapeDtypeStruct((t, t), bf16),
            jax.ShapeDtypeStruct((t, n), bf16),
            jax.ShapeDtypeStruct((n, t), bf16),
            jax.ShapeDtypeStruct((n, n), bf16),
        ),
        in_specs=[VM] * 5,
        out_specs=(VM,) * 5,
        name="update",
    )(state, own, right, low, diag)


def tile_sum(part):
    peers = lax.axis_size("tile")
    shape = part.shape
    rows = part.reshape(peers, -1, shape[-1]).astype(bf16)
    got = lax.all_to_all(rows, "tile", 0, 0, tiled=True)
    mine = jnp.sum(got.astype(f32), 0).astype(bf16)
    wide = jnp.broadcast_to(mine[None], rows.shape)
    return lax.all_to_all(wide, "tile", 0, 0, tiled=True).reshape(shape)


def body(obj, probe, mode_weights, measured, corner, counts, weight_index):
    n = probe.shape[-1]
    t = obj.shape[-1]
    me = lax.axis_index("mode")
    one, two = dft_tables(n)
    positions = POS_DEV * lax.axis_size("tile")
    info = jnp.stack([me.astype(jnp.int32), counts[0]])
    state = lax.dynamic_index_in_dim(obj[0], me, 0, keepdims=False)
    rest = lax.dynamic_index_in_dim(obj[0], 1 - me, 0, keepdims=False).astype(bf16)
    half = state.astype(bf16)
    edges = (half[:, :n], half[:n, :], half[:n, :n])
    pm = probe
    po = swapped(probe)
    wm = mode_weights
    wo = swapped(mode_weights)
    for sweep in range(ITERS):
        right = shifted(edges[0], -1)
        low = shifted(edges[1], -GC)
        diag = shifted(edges[2], -(GC + 1))
        mine = (half, right, low, diag)
        other = (rest, swapped(right), swapped(low), swapped(diag))
        keep, send, pgm, pgo = patches(
            info, corner, weight_index, wm, wo, mine, other, measured, pm, po, one, two
        )
        probe_grad = tile_sum(pgm + swapped(pgo).astype(f32))
        own, right, low, diag = margins(keep, swapped(send), t)
        right = shifted(right, 1)
        low = shifted(low, GC)
        diag = shifted(diag, GC + 1)
        state, half, *edges = update(state, own, right, low, diag)
        rate = step_probe / positions
        pm = pm - rate * probe_grad.astype(f32)
        if sweep < ITERS - 1:
            rest = swapped(half)
            po = po - rate * swapped(probe_grad).astype(f32)
    rest = swapped(state)
    first = jnp.where(me == 0, state, rest)
    second = jnp.where(me == 0, rest, state)
    return (jnp.stack([first, second])[None], pm)


def solution(mesh):
    placed = (
        P("tile", None, None, None),
        P("mode", None, None, None),
        P(None, "mode"),
        P("tile", None, None),
        P("tile", None),
        P("tile"),
        P("tile"),
    )
    return jax.shard_map(
        body,
        mesh=mesh,
        in_specs=placed,
        out_specs=(P("tile", None, None, None), P("mode", None, None, None)),
        check_vma=False,
    )
```

time: 581 us -> 204 us (0.35)
  blocking collectives: 196 us -> 18.1 us
  local copies, waits for them, and re-layouts: 107 us -> 10.7 us
  waiting for transfers between devices: 129 us -> 74.8 us
  other arithmetic: 61 us -> 14 us
  Pallas kernels: 0 us -> 36.6 us
  matrix products: 22 us -> 0 us
  starting transfers between devices: 29.3 us -> 46.3 us
  loops' own time: 15.8 us -> 0 us
  between operations: 15.9 us -> 1.68 us
    psum x2 -> x0, blocking collectives: 194 us -> none  [body(): probe_grad = lax.psum(probe_updates, 'tile')]
    pallas_call x0 -> x6, Pallas kernels: none -> 36.6 us  [the longest x2 25.9 us: patches(): pl.pallas_call(patch_kernel, out_shape=(jax.ShapeDtypeStruct((f, f), f32)...]
    ppermute x12 -> x27, waiting for transfers between devices: 83.4 us -> 49.5 us  [the longest x12 43.4 us: shifted(): lax.ppermute(array, 'tile', [(i, (i + by) % peers) for i in range(peers)])]
    psum x2 -> x0, waiting for transfers between devices: 32.8 us -> none  [body(): lax.psum(tile_grad.astype(jnp.bfloat16), 'mode').astype(jnp.float32)]
    another operation x13 -> x4, other arithmetic: 32 us -> 2.78 us
    dynamic_update_slice x4 -> x0, local copies, waits for them, and re-layouts: 25.4 us -> none  [place(): return lax.dynamic_update_slice(acc, current + object_terms[slot], where)]
    all_to_all x0 -> x3, waiting for transfers between devices: none -> 25.3 us  [the longest x2 25.3 us: tile_sum(): return lax.all_to_all(wide, 'tile', 0, 0, tiled=True).reshape(shape)]
    dot_general x9 -> x0, matrix products: 22 us -> none  [the longest x4 16.8 us: transform(): jnp.einsum('ij,bjk->bik', left, field.reshape(count, 2 * length, length),...]
  transfers between devices with their start and end apart: 18 -> 30, of which waited for: 10 -> 11; matrix products, arithmetic and copies ran while one was open for 8% -> 8% of each run, Pallas kernels for 0% -> 5%
where the time goes in v1:
time: 204 us; the launch traced here: 202 us
  waiting for transfers between devices  74.8 us (37%)
  starting transfers between devices  46.3 us (23%)
  Pallas kernels  36.6 us (18%)
  blocking collectives  18.1 us (9%)
  other arithmetic  14 us (7%)
  local copies, waits for them, and re-layouts  10.7 us (5%)
    ppermute x12, waiting for transfers between devices, shifted(): lax.ppermute(array, 'tile', [(i, (i + by) % peers) for i in range(peers)])  43.4 us
    ppermute x12, starting transfers between devices, shifted(): lax.ppermute(array, 'tile', [(i, (i + by) % peers) for i in range(peers)])  27.7 us
    pallas_call x2, Pallas kernels, patches(): pl.pallas_call(patch_kernel, out_shape=(jax.ShapeDtypeStruct((f, f), f32)...  25.9 us
    all_to_all x2, waiting for transfers between devices, tile_sum(): return lax.all_to_all(wide, 'tile', 0, 0, tiled=True).reshape(shape)  25.3 us
    all_to_all x1, blocking collectives, tile_sum(): got = lax.all_to_all(rows, 'tile', 0, 0, tiled=True)  18.1 us
    all_to_all x2, starting transfers between devices, tile_sum(): return lax.all_to_all(wide, 'tile', 0, 0, tiled=True).reshape(shape)  12.8 us
    unnamed x64, local copies, waits for them, and re-layouts  7.15 us
    ppermute x15, waiting for transfers between devices, swapped(): return lax.ppermute(array, 'mode', [(0, 1), (1, 0)])  6.07 us
  transfers between devices with their start and end apart: 30, of which 11 were waited for; matrix products, arithmetic and copies ran while one was open for 8% of the time, Pallas kernels for 5%

profile of v1, /device:TPU:0, one launch (start us, length us, event | category | flops | bytes accessed | tf_op | source)
XLA Modules:
  0.0 202.3 jit_solution(4750863039562163596)
XLA Ops:
  1.2 0.8 copy.11.wm
  2.0 2.0 fusion.10
  3.9 5.0 %collective-permute-start.3 = (bf16[256,256]{1,0:T(8,128)(2,1)S(1)}, bf16[256,256]{1,0:T(8,128)(2,1)S(1)}, u32[]{:S(2)}, u32[]{:S(2)}) collective-permute-start(bf16[256,256]{1,0:T(8,128)(2,1)S(1)} %slice.14), channel_id=1, source_target_pairs={{0,14},{2,16},{4,18},{6,20},{8,22},{10,24},{12,26},{14,28},{16,30}... | collective-permute-start | bytes 393224 | tf_op jit(solution)/shard_map/ppermute | solution.py:27
  8.9 2.4 %collective-permute-start.1 = (bf16[384,256]{1,0:T(8,128)(2,1)S(1)}, bf16[384,256]{1,0:T(8,128)(2,1)S(1)}, u32[]{:S(2)}, u32[]{:S(2)}) collective-permute-start(bf16[384,256]{1,0:T(8,128)(2,1)S(1)} %slice.12), channel_id=1, source_target_pairs={{0,30},{2,0},{4,2},{6,4},{8,6},{10,8},{12,10},{14,12},{16,14},{18,... | collective-permute-start | bytes 589832 | tf_op jit(solution)/shard_map/ppermute | solution.py:27
  11.4 1.8 collective-permute-start.2
  13.1 1.8 fusion.2.to
  15.0 1.1 negate_convert_fusion
  16.1 1.0 fusion.9
  17.8 9.4 %collective-permute-done.2.bm = bf16[256,384]{1,0:T(8,128)(2,1)S(1)} collective-permute-done((bf16[256,384]{1,0:T(8,128)(2,1)S(1)}, bf16[256,384]{1,0:T(8,128)(2,1)S(1)}, u32[]{:S(2)}, u32[]{:S(2)}) %collective-permute-start.2) | collective-permute-done | bytes 196640 | tf_op jit(solution)/shard_map/ppermute | solution.py:27
  28.3 1.1 fusion.1
  31.2 13.0 %patch.2 = (f32[640,640]{1,0:T(8,128)}, bf16[640,640]{1,0:T(8,128)(2,1)}, f32[2,2,256,256]{3,2,1,0:T(8,128)}, bf16[2,2,256,256]{3,2,1,0:T(8,128)(2,1)}) custom-call(s32[2]{0:T(128)} %pad_add_fusion.info, s32[4,2]{1,0:T(4,128)} %copy.10.corner, s32[4]{0:T(128)} %kind.3, f32[8,2]{1,0:T(8,128)} %copy-done.27, f32[8,2]{1,0:T(8,128)} %copy-done.28, ...), custom_call_target="tpu_custom_call" | custom-call | tf_op jit(solution)/shard_map/patch/pallas_call | solution.py:166
  44.2 2.1 %collective-permute-done.19 = bf16[2,2,256,256]{3,2,1,0:T(8,128)(2,1)S(1)} collective-permute-done((bf16[2,2,256,256]{3,2,1,0:T(8,128)(2,1)}, bf16[2,2,256,256]{3,2,1,0:T(8,128)(2,1)S(1)}, u32[]{:S(2)}, u32[]{:S(2)}) %collective-permute-start.19) | collective-permute-done | bytes 524320 | tf_op jit(solution)/shard_map/ppermute | solution.py:36
  46.3 1.3 add_convert_fusion.1
  47.7 18.1 %all_to_all.20 = bf16[16,64,256]{2,1,0:T(8,128)(2,1)S(1)} all-to-all(bf16[16,64,256]{2,1,0:T(8,128)(2,1)S(1)} %bitcast.19), channel_id=1, replica_groups=mesh['tile'=16,'mode'=2] {'tile'}, dimensions={0} | all-to-all | bytes 1048576 | tf_op jit(solution)/shard_map/all_to_all | solution.py:255
  65.9 0.9 broadcast_in_dim.6
  66.7 4.1 %all-to-all-start.1 = ((bf16[16,64,256]{2,1,0:T(8,128)(2,1)}), bf16[16,64,256]{2,1,0:T(8,128)(2,1)S(1)}, u32[]{:S(2)}, u32[]{:S(2)}) async-start(bf16[16,64,256]{2,1,0:T(8,128)(2,1)} %broadcast_in_dim.6), calls=%async_computation.1 | async-start | bytes 1048576 | tf_op jit(solution)/shard_map/all_to_all | solution.py:258
  70.9 2.3 %collective-permute-done.8.got = bf16[640,640]{1,0:T(8,128)(2,1)S(1)} collective-permute-done((bf16[640,640]{1,0:T(8,128)(2,1)S(1)}, bf16[640,640]{1,0:T(8,128)(2,1)S(1)}, u32[]{:S(2)}, u32[]{:S(2)}) %collective-permute-start.8) | collective-permute-done | bytes 819232 | tf_op jit(solution)/shard_map/ppermute | solution.py:36
  73.2 0.9 copy-done.6
  74.1 2.7 %margin.2 = (f32[384,384]{1,0:T(8,128)}, bf16[384,256]{1,0:T(8,128)(2,1)}, bf16[256,384]{1,0:T(8,128)(2,1)}, bf16[256,256]{1,0:T(8,128)(2,1)}) custom-call(f32[640,640]{1,0:T(8,128)} %get-tuple-element.24.keep, bf16[640,640]{1,0:T(8,128)(2,1)} %copy-done.6), custom_call_target="tpu_custom_call" | custom-call | tf_op jit(solution)/shard_map/margin/pallas_call | solution.py:204
  76.8 1.9 collective-permute-start.9
  78.7 2.4 %collective-permute-start.10 = (bf16[256,384]{1,0:T(8,128)(2,1)}, bf16[256,384]{1,0:T(8,128)(2,1)S(1)}, u32[]{:S(2)}, u32[]{:S(2)}) collective-permute-start(bf16[256,384]{1,0:T(8,128)(2,1)} %get-tuple-element.28), channel_id=1, source_target_pairs={{0,16},{2,18},{4,20},{6,22},{8,24},{10,26},{12,28},{14,30},{16,0},... | collective-permute-start | bytes 589832 | tf_op jit(solution)/shard_map/ppermute | solution.py:27
  81.1 1.5 collective-permute-start.11
  82.5 11.0 %all-to-all-done.1 = bf16[16,64,256]{2,1,0:T(8,128)(2,1)S(1)} async-done(((bf16[16,64,256]{2,1,0:T(8,128)(2,1)}), bf16[16,64,256]{2,1,0:T(8,128)(2,1)S(1)}, u32[]{:S(2)}, u32[]{:S(2)}) %all-to-all-start.1) | async-done | bytes 524320 | tf_op jit(solution)/shard_map/all_to_all | solution.py:258
  93.5 3.1 %collective-permute-done.10.low = bf16[256,384]{1,0:T(8,128)(2,1)S(1)} collective-permute-done((bf16[256,384]{1,0:T(8,128)(2,1)}, bf16[256,384]{1,0:T(8,128)(2,1)S(1)}, u32[]{:S(2)}, u32[]{:S(2)}) %collective-permute-start.10) | collective-permute-done | bytes 196640 | tf_op jit(solution)/shard_map/ppermute | solution.py:27
  97.3 2.7 %update.2 = (f32[384,384]{1,0:T(8,128)}, bf16[384,384]{1,0:T(8,128)(2,1)}, bf16[384,256]{1,0:T(8,128)(2,1)}, bf16[256,384]{1,0:T(8,128)(2,1)}, bf16[256,256]{1,0:T(8,128)(2,1)}) custom-call(f32[384,384]{1,0:T(8,128)} %get-tuple-element.47.state, f32[384,384]{1,0:T(8,128)} %get-tuple-element.26.own, bf16[384,256]{1,0:T(8,128)(2,1)} %copy-done.17, ...), custom_call_target="tpu_custom_call" | custom-call | tf_op jit(solution)/shard_map/update/pallas_call | solution.py:236
  100.0 6.5 %collective-permute-start.12 = (bf16[384,256]{1,0:T(8,128)(2,1)}, bf16[384,256]{1,0:T(8,128)(2,1)S(1)}, u32[]{:S(2)}, u32[]{:S(2)}) collective-permute-start(bf16[384,256]{1,0:T(8,128)(2,1)} %get-tuple-element.32), channel_id=1, source_target_pairs={{0,30},{2,0},{4,2},{6,4},{8,6},{10,8},{12,10},{14,12},{16,14},{18,... | collective-permute-start | bytes 589832 | tf_op jit(solution)/shard_map/ppermute | solution.py:27
  106.6 0.7 collective-permute-start.14
  107.2 12.5 %collective-permute-done.14.dm = bf16[256,256]{1,0:T(8,128)(2,1)S(1)} collective-permute-done((bf16[256,256]{1,0:T(8,128)(2,1)}, bf16[256,256]{1,0:T(8,128)(2,1)S(1)}, u32[]{:S(2)}, u32[]{:S(2)}) %collective-permute-start.14) | collective-permute-done | bytes 131104 | tf_op jit(solution)/shard_map/ppermute | solution.py:27
  120.9 1.1 multiply_subtract_fusion.1.pm
  122.1 1.1 multiply_subtract_fusion.po
  124.0 0.7 copy-done.16
  124.7 13.0 %patch.3 = (f32[640,640]{1,0:T(8,128)}, bf16[640,640]{1,0:T(8,128)(2,1)}, f32[2,2,256,256]{3,2,1,0:T(8,128)}, bf16[2,2,256,256]{3,2,1,0:T(8,128)(2,1)}) custom-call(s32[2]{0:T(128)} %pad_add_fusion.info, s32[4,2]{1,0:T(4,128)} %copy.10.corner, s32[4]{0:T(128)} %kind.3, f32[8,2]{1,0:T(8,128)} %copy-done.27, f32[8,2]{1,0:T(8,128)} %copy-done.28, ...), custom_call_target="tpu_custom_call" | custom-call | tf_op jit(solution)/shard_map/patch/pallas_call | solution.py:166
  138.2 1.6 collective-permute-done.26
  139.8 2.2 %add_convert_fusion = bf16[2,2,256,256]{3,2,1,0:T(8,128)(2,1)} fusion(f32[2,2,256,256]{3,2,1,0:T(8,128)} %get-tuple-element.44, bf16[2,2,256,256]{3,2,1,0:T(8,128)(2,1)S(1)} %collective-permute-done.26), kind=kLoop, calls=%fused_computation.2 | loop fusion | flops 786432 | bytes 2097152 | tf_op jit(solution)/shard_map/convert_element_type | solution.py:254
  141.9 3.6 %all-to-all-start.2 = ((bf16[16,64,256]{2,1,0:T(8,128)(2,1)}), bf16[16,64,256]{2,1,0:T(8,128)(2,1)S(1)}, u32[]{:S(2)}, u32[]{:S(2)}) async-start(bf16[16,64,256]{2,1,0:T(8,128)(2,1)} %bitcast.8), calls=%async_computation.2 | async-start | bytes 1048576 | tf_op jit(solution)/shard_map/all_to_all | solution.py:255
  145.6 0.9 copy-done.5
  146.4 2.7 %margin.3 = (f32[384,384]{1,0:T(8,128)}, bf16[384,256]{1,0:T(8,128)(2,1)}, bf16[256,384]{1,0:T(8,128)(2,1)}, bf16[256,256]{1,0:T(8,128)(2,1)}) custom-call(f32[640,640]{1,0:T(8,128)} %get-tuple-element.37.keep, bf16[640,640]{1,0:T(8,128)(2,1)} %copy-done.5), custom_call_target="tpu_custom_call" | custom-call | tf_op jit(solution)/shard_map/margin/pallas_call | solution.py:204
  149.1 1.8 collective-permute-start.22
  150.9 2.4 %collective-permute-start.23 = (bf16[256,384]{1,0:T(8,128)(2,1)}, bf16[256,384]{1,0:T(8,128)(2,1)S(1)}, u32[]{:S(2)}, u32[]{:S(2)}) collective-permute-start(bf16[256,384]{1,0:T(8,128)(2,1)} %get-tuple-element.41), channel_id=1, source_target_pairs={{0,16},{2,18},{4,20},{6,22},{8,24},{10,26},{12,28},{14,30},{16,0},... | collective-permute-start | bytes 589832 | tf_op jit(solution)/shard_map/ppermute | solution.py:27
  153.3 1.4 collective-permute-start.24
  154.7 11.0 %collective-permute-done.24.diag = bf16[256,256]{1,0:T(8,128)(2,1)S(1)} collective-permute-done((bf16[256,256]{1,0:T(8,128)(2,1)}, bf16[256,256]{1,0:T(8,128)(2,1)S(1)}, u32[]{:S(2)}, u32[]{:S(2)}) %collective-permute-start.24) | collective-permute-done | bytes 131104 | tf_op jit(solution)/shard_map/ppermute | solution.py:27
  165.8 6.7 %collective-permute-done.23.low = bf16[256,384]{1,0:T(8,128)(2,1)S(1)} collective-permute-done((bf16[256,384]{1,0:T(8,128)(2,1)}, bf16[256,384]{1,0:T(8,128)(2,1)S(1)}, u32[]{:S(2)}, u32[]{:S(2)}) %collective-permute-start.23) | collective-permute-done | bytes 196640 | tf_op jit(solution)/shard_map/ppermute | solution.py:27
  173.2 2.7 %update.3 = (f32[384,384]{1,0:T(8,128)}, bf16[384,384]{1,0:T(8,128)(2,1)}, bf16[384,256]{1,0:T(8,128)(2,1)}, bf16[256,384]{1,0:T(8,128)(2,1)}, bf16[256,256]{1,0:T(8,128)(2,1)}) custom-call(f32[384,384]{1,0:T(8,128)} %get-tuple-element.30.state, f32[384,384]{1,0:T(8,128)} %get-tuple-element.39.own, bf16[384,256]{1,0:T(8,128)(2,1)} %copy-done.19, ...), custom_call_target="tpu_custom_call" | custom-call | tf_op jit(solution)/shard_map/update/pallas_call | solution.py:236
  175.9 0.9 broadcast_in_dim.8
  176.8 8.7 %all-to-all-start.3 = ((bf16[16,64,256]{2,1,0:T(8,128)(2,1)}), bf16[16,64,256]{2,1,0:T(8,128)(2,1)S(1)}, u32[]{:S(2)}, u32[]{:S(2)}) async-start(bf16[16,64,256]{2,1,0:T(8,128)(2,1)} %broadcast_in_dim.8), calls=%async_computation.3 | async-start | bytes 1048576 | tf_op jit(solution)/shard_map/all_to_all | solution.py:258
  185.6 1.1 maximum_bitcast_fusion
  186.7 14.3 %all-to-all-done.3 = bf16[16,64,256]{2,1,0:T(8,128)(2,1)S(1)} async-done(((bf16[16,64,256]{2,1,0:T(8,128)(2,1)}), bf16[16,64,256]{2,1,0:T(8,128)(2,1)S(1)}, u32[]{:S(2)}, u32[]{:S(2)}) %all-to-all-start.3) | async-done | bytes 524320 | tf_op jit(solution)/shard_map/all_to_all | solution.py:258
  201.1 1.1 sub.15
  (104 shorter events, 7.9 us)
Async XLA Ops:
  0.6 29.5 %collective-permute-start.7 = (f32[2,2,256,256]{3,2,1,0:T(8,128)}, f32[2,2,256,256]{3,2,1,0:T(8,128)S(1)}, u32[]{:S(2)}, u32[]{:S(2)}) collective-permute-start(f32[2,2,256,256]{3,2,1,0:T(8,128)} %pm.1), channel_id=1, source_target_pairs={{0,1},{1,0},{2,3},{3,2},{4,5},{5,4},{6,7},{7,6},{8,9},{9,8},{10,11... | collective-permute-start | bytes 3145736 | tf_op jit(solution)/shard_map/ppermute | solution.py:36
  1.9 9.4 %copy-start.27 = (f32[8,2]{1,0:T(8,128)}, f32[8,2]{1,0:T(8,128)S(1)}, u32[]{:S(2)}) copy-start(f32[8,2]{1,0:T(8,128)S(1)} %copy.11.wm) | copy-start | bytes 196
  1.9 28.2 %collective-permute-start = (f32[8,2]{1,0:T(8,128)S(1)}, f32[8,2]{1,0:T(8,128)S(1)}, u32[]{:S(2)}, u32[]{:S(2)}) collective-permute-start(f32[8,2]{1,0:T(8,128)S(1)} %copy.11.wm), channel_id=1, source_target_pairs={{0,1},{1,0},{2,3},{3,2},{4,5},{5,4},{6,7},{7,6},{8,9},{9,8},{10,11... | collective-permute-start | bytes 200 | tf_op jit(solution)/shard_map/ppermute | solution.py:36
  3.9 25.5 %copy-start.1 = (bf16[384,384]{1,0:T(8,128)(2,1)}, bf16[384,384]{1,0:T(8,128)(2,1)S(1)}, u32[]{:S(2)}) copy-start(bf16[384,384]{1,0:T(8,128)(2,1)S(1)} %get-tuple-element.46.tm) | copy-start | bytes 884740
  3.9 23.9 %collective-permute-start.3 = (bf16[256,256]{1,0:T(8,128)(2,1)S(1)}, bf16[256,256]{1,0:T(8,128)(2,1)S(1)}, u32[]{:S(2)}, u32[]{:S(2)}) collective-permute-start(bf16[256,256]{1,0:T(8,128)(2,1)S(1)} %slice.14), channel_id=1, source_target_pairs={{0,14},{2,16},{4,18},{6,20},{8,22},{10,24},{12,26},{14,28},{16,30}... | collective-permute-start | bytes 393224 | tf_op jit(solution)/shard_map/ppermute | solution.py:27
  8.9 8.8 %collective-permute-start.1 = (bf16[384,256]{1,0:T(8,128)(2,1)S(1)}, bf16[384,256]{1,0:T(8,128)(2,1)S(1)}, u32[]{:S(2)}, u32[]{:S(2)}) collective-permute-start(bf16[384,256]{1,0:T(8,128)(2,1)S(1)} %slice.12), channel_id=1, source_target_pairs={{0,30},{2,0},{4,2},{6,4},{8,6},{10,8},{12,10},{14,12},{16,14},{18,... | collective-permute-start | bytes 589832 | tf_op jit(solution)/shard_map/ppermute | solution.py:27
  11.4 15.8 %collective-permute-start.2 = (bf16[256,384]{1,0:T(8,128)(2,1)S(1)}, bf16[256,384]{1,0:T(8,128)(2,1)S(1)}, u32[]{:S(2)}, u32[]{:S(2)}) collective-permute-start(bf16[256,384]{1,0:T(8,128)(2,1)S(1)} %slice.13), channel_id=1, source_target_pairs={{0,16},{2,18},{4,20},{6,22},{8,24},{10,26},{12,28},{14,30},{16,0},... | collective-permute-start | bytes 589832 | tf_op jit(solution)/shard_map/ppermute | solution.py:27
  13.1 16.3 %copy-start.29 = (s32[4,2]{0,1:T(2,128)S(1)}, s32[4,2]{0,1:T(2,128)}, u32[]{:S(2)}) copy-start(s32[4,2]{0,1:T(2,128)} %param.11) | copy-start | bytes 100
  17.7 12.5 %copy-start.9 = (bf16[384,256]{1,0:T(8,128)(2,1)}, bf16[384,256]{1,0:T(8,128)(2,1)S(1)}, u32[]{:S(2)}) copy-start(bf16[384,256]{1,0:T(8,128)(2,1)S(1)} %collective-permute-done.1.rm) | copy-start | bytes 589828
  17.7 12.4 %collective-permute-start.4 = (bf16[384,256]{1,0:T(8,128)(2,1)S(1)}, bf16[384,256]{1,0:T(8,128)(2,1)S(1)}, u32[]{:S(2)}, u32[]{:S(2)}) collective-permute-start(bf16[384,256]{1,0:T(8,128)(2,1)S(1)} %collective-permute-done.1.rm), channel_id=1, source_target_pairs={{0,1},{1,0},{2,3},{3,2},{4,5},{5,4},{6,7},{7,6},{8,9},{9,8},{10,11... | collective-permute-start | bytes 589832 | tf_op jit(solution)/shard_map/ppermute | solution.py:36
  27.2 3.0 %copy-start.10 = (bf16[256,384]{1,0:T(8,128)(2,1)}, bf16[256,384]{1,0:T(8,128)(2,1)S(1)}, u32[]{:S(2)}) copy-start(bf16[256,384]{1,0:T(8,128)(2,1)S(1)} %collective-permute-done.2.bm) | copy-start | bytes 589828
  27.2 2.9 %collective-permute-start.5 = (bf16[256,384]{1,0:T(8,128)(2,1)S(1)}, bf16[256,384]{1,0:T(8,128)(2,1)S(1)}, u32[]{:S(2)}, u32[]{:S(2)}) collective-permute-start(bf16[256,384]{1,0:T(8,128)(2,1)S(1)} %collective-permute-done.2.bm), channel_id=1, source_target_pairs={{0,1},{1,0},{2,3},{3,2},{4,5},{5,4},{6,7},{7,6},{8,9},{9,8},{10,11... | collective-permute-start | bytes 589832 | tf_op jit(solution)/shard_map/ppermute | solution.py:36
  27.8 2.4 %copy-start.21 = (bf16[256,256]{1,0:T(8,128)(2,1)}, bf16[256,256]{1,0:T(8,128)(2,1)S(1)}, u32[]{:S(2)}) copy-start(bf16[256,256]{1,0:T(8,128)(2,1)S(1)} %collective-permute-done.3.dm) | copy-start | bytes 393220
  27.8 2.3 %collective-permute-start.6 = (bf16[256,256]{1,0:T(8,128)(2,1)S(1)}, bf16[256,256]{1,0:T(8,128)(2,1)S(1)}, u32[]{:S(2)}, u32[]{:S(2)}) collective-permute-start(bf16[256,256]{1,0:T(8,128)(2,1)S(1)} %collective-permute-done.3.dm), channel_id=1, source_target_pairs={{0,1},{1,0},{2,3},{3,2},{4,5},{5,4},{6,7},{7,6},{8,9},{9,8},{10,11... | collective-permute-start | bytes 393224 | tf_op jit(solution)/shard_map/ppermute | solution.py:36
  44.2 2.1 %collective-permute-start.19 = (bf16[2,2,256,256]{3,2,1,0:T(8,128)(2,1)}, bf16[2,2,256,256]{3,2,1,0:T(8,128)(2,1)S(1)}, u32[]{:S(2)}, u32[]{:S(2)}) collective-permute-start(bf16[2,2,256,256]{3,2,1,0:T(8,128)(2,1)} %get-tuple-element.36), channel_id=1, source_target_pairs={{0,1},{1,0},{2,3},{3,2},{4,5},{5,4},{6,7},{7,6},{8,9},{9,8},{10,11... | collective-permute-start | bytes 1572872 | tf_op jit(solution)/shard_map/ppermute | solution.py:36
  65.8 5.0 %copy-start.30 = (bf16[640,640]{1,0:T(8,128)(2,1)S(1)}, bf16[640,640]{1,0:T(8,128)(2,1)}, u32[]{:S(2)}) copy-start(bf16[640,640]{1,0:T(8,128)(2,1)} %get-tuple-element.25) | copy-start | bytes 2457604
  66.7 26.8 %all-to-all-start.1 = ((bf16[16,64,256]{2,1,0:T(8,128)(2,1)}), bf16[16,64,256]{2,1,0:T(8,128)(2,1)S(1)}, u32[]{:S(2)}, u32[]{:S(2)}) async-start(bf16[16,64,256]{2,1,0:T(8,128)(2,1)} %broadcast_in_dim.6), calls=%async_computation.1 | async-start | bytes 1048576 | tf_op jit(solution)/shard_map/all_to_all | solution.py:258
  70.8 2.4 %collective-permute-start.8 = (bf16[640,640]{1,0:T(8,128)(2,1)S(1)}, bf16[640,640]{1,0:T(8,128)(2,1)S(1)}, u32[]{:S(2)}, u32[]{:S(2)}) collective-permute-start(bf16[640,640]{1,0:T(8,128)(2,1)S(1)} %copy-done.30), channel_id=1, source_target_pairs={{0,1},{1,0},{2,3},{3,2},{4,5},{5,4},{6,7},{7,6},{8,9},{9,8},{10,11... | collective-permute-start | bytes 2457608 | tf_op jit(solution)/shard_map/ppermute | solution.py:36
  76.8 44.1 %copy-start.2 = (f32[2,2,256,256]{3,2,1,0:T(8,128)S(1)}, f32[2,2,256,256]{3,2,1,0:T(8,128)}, u32[]{:S(2)}) copy-start(f32[2,2,256,256]{3,2,1,0:T(8,128)} %pm.1) | copy-start | bytes 3145732
  76.8 16.7 %collective-permute-start.9 = (bf16[384,256]{1,0:T(8,128)(2,1)}, bf16[384,256]{1,0:T(8,128)(2,1)S(1)}, u32[]{:S(2)}, u32[]{:S(2)}) collective-permute-start(bf16[384,256]{1,0:T(8,128)(2,1)} %get-tuple-element.27), channel_id=1, source_target_pairs={{0,2},{2,4},{4,6},{6,8},{8,10},{10,12},{12,14},{14,16},{16,18},{18... | collective-permute-start | bytes 589832 | tf_op jit(solution)/shard_map/ppermute | solution.py:27
  78.7 17.9 %collective-permute-start.10 = (bf16[256,384]{1,0:T(8,128)(2,1)}, bf16[256,384]{1,0:T(8,128)(2,1)S(1)}, u32[]{:S(2)}, u32[]{:S(2)}) collective-permute-start(bf16[256,384]{1,0:T(8,128)(2,1)} %get-tuple-element.28), channel_id=1, source_target_pairs={{0,16},{2,18},{4,20},{6,22},{8,24},{10,26},{12,28},{14,30},{16,0},... | collective-permute-start | bytes 589832 | tf_op jit(solution)/shard_map/ppermute | solution.py:27
  81.1 12.4 %collective-permute-start.11 = (bf16[256,256]{1,0:T(8,128)(2,1)}, bf16[256,256]{1,0:T(8,128)(2,1)S(1)}, u32[]{:S(2)}, u32[]{:S(2)}) collective-permute-start(bf16[256,256]{1,0:T(8,128)(2,1)} %get-tuple-element.29), channel_id=1, source_target_pairs={{0,18},{2,20},{4,22},{6,24},{8,26},{10,28},{12,30},{14,0},{16,2},{... | collective-permute-start | bytes 393224 | tf_op jit(solution)/shard_map/ppermute | solution.py:27
  93.5 28.5 %collective-permute-start.20 = (bf16[2,2,256,256]{3,2,1,0:T(8,128)(2,1)S(1)}, bf16[2,2,256,256]{3,2,1,0:T(8,128)(2,1)S(1)}, u32[]{:S(2)}, u32[]{:S(2)}) collective-permute-start(bf16[2,2,256,256]{3,2,1,0:T(8,128)(2,1)S(1)} %bitcast.17), channel_id=1, source_target_pairs={{0,1},{1,0},{2,3},{3,2},{4,5},{5,4},{6,7},{7,6},{8,9},{9,8},{10,11... | collective-permute-start | bytes 1572872 | tf_op jit(solution)/shard_map/ppermute | solution.py:36
  93.5 3.1 %copy-start.25 = (bf16[256,256]{1,0:T(8,128)(2,1)}, bf16[256,256]{1,0:T(8,128)(2,1)S(1)}, u32[]{:S(2)}) copy-start(bf16[256,256]{1,0:T(8,128)(2,1)S(1)} %collective-permute-done.11.diag) | copy-start | bytes 393220
  93.5 3.1 %copy-start.17 = (bf16[384,256]{1,0:T(8,128)(2,1)}, bf16[384,256]{1,0:T(8,128)(2,1)S(1)}, u32[]{:S(2)}) copy-start(bf16[384,256]{1,0:T(8,128)(2,1)S(1)} %collective-permute-done.9.right) | copy-start | bytes 589828
  100.0 19.7 %collective-permute-start.12 = (bf16[384,256]{1,0:T(8,128)(2,1)}, bf16[384,256]{1,0:T(8,128)(2,1)S(1)}, u32[]{:S(2)}, u32[]{:S(2)}) collective-permute-start(bf16[384,256]{1,0:T(8,128)(2,1)} %get-tuple-element.32), channel_id=1, source_target_pairs={{0,30},{2,0},{4,2},{6,4},{8,6},{10,8},{12,10},{14,12},{16,14},{18,... | collective-permute-start | bytes 589832 | tf_op jit(solution)/shard_map/ppermute | solution.py:27
  106.6 14.4 %collective-permute-start.13 = (bf16[256,384]{1,0:T(8,128)(2,1)}, bf16[256,384]{1,0:T(8,128)(2,1)S(1)}, u32[]{:S(2)}, u32[]{:S(2)}) collective-permute-start(bf16[256,384]{1,0:T(8,128)(2,1)} %get-tuple-element.33), channel_id=1, source_target_pairs={{0,16},{2,18},{4,20},{6,22},{8,24},{10,26},{12,28},{14,30},{16,0},... | collective-permute-start | bytes 589832 | tf_op jit(solution)/shard_map/ppermute | solution.py:27
  106.6 13.2 %collective-permute-start.14 = (bf16[256,256]{1,0:T(8,128)(2,1)}, bf16[256,256]{1,0:T(8,128)(2,1)S(1)}, u32[]{:S(2)}, u32[]{:S(2)}) collective-permute-start(bf16[256,256]{1,0:T(8,128)(2,1)} %get-tuple-element.34), channel_id=1, source_target_pairs={{0,14},{2,16},{4,18},{6,20},{8,22},{10,24},{12,26},{14,28},{16,30}... | collective-permute-start | bytes 393224 | tf_op jit(solution)/shard_map/ppermute | solution.py:27
  107.2 14.8 %copy-start.4 = (f32[2,2,256,256]{3,2,1,0:T(8,128)S(1)}, f32[2,2,256,256]{3,2,1,0:T(8,128)}, u32[]{:S(2)}) copy-start(f32[2,2,256,256]{3,2,1,0:T(8,128)} %copy-done.3) | copy-start | bytes 3145732
  107.2 15.9 %collective-permute-start.15 = (bf16[384,384]{1,0:T(8,128)(2,1)}, bf16[384,384]{1,0:T(8,128)(2,1)S(1)}, u32[]{:S(2)}, u32[]{:S(2)}) collective-permute-start(bf16[384,384]{1,0:T(8,128)(2,1)} %get-tuple-element.31.tm), channel_id=1, source_target_pairs={{0,1},{1,0},{2,3},{3,2},{4,5},{5,4},{6,7},{7,6},{8,9},{9,8},{10,11... | collective-permute-start | bytes 884744 | tf_op jit(solution)/shard_map/ppermute | solution.py:36
  119.7 2.3 %copy-start.22 = (bf16[256,256]{1,0:T(8,128)(2,1)}, bf16[256,256]{1,0:T(8,128)(2,1)S(1)}, u32[]{:S(2)}) copy-start(bf16[256,256]{1,0:T(8,128)(2,1)S(1)} %collective-permute-done.14.dm) | copy-start | bytes 393220
  119.7 3.4 %collective-permute-start.18 = (bf16[256,256]{1,0:T(8,128)(2,1)S(1)}, bf16[256,256]{1,0:T(8,128)(2,1)S(1)}, u32[]{:S(2)}, u32[]{:S(2)}) collective-permute-start(bf16[256,256]{1,0:T(8,128)(2,1)S(1)} %collective-permute-done.14.dm), channel_id=1, source_target_pairs={{0,1},{1,0},{2,3},{3,2},{4,5},{5,4},{6,7},{7,6},{8,9},{9,8},{10,11... | collective-permute-start | bytes 393224 | tf_op jit(solution)/shard_map/ppermute | solution.py:36
  119.7 2.3 %copy-start.11 = (bf16[384,256]{1,0:T(8,128)(2,1)}, bf16[384,256]{1,0:T(8,128)(2,1)S(1)}, u32[]{:S(2)}) copy-start(bf16[384,256]{1,0:T(8,128)(2,1)S(1)} %collective-permute-done.12.rm) | copy-start | bytes 589828
  119.7 3.4 %collective-permute-start.16 = (bf16[384,256]{1,0:T(8,128)(2,1)S(1)}, bf16[384,256]{1,0:T(8,128)(2,1)S(1)}, u32[]{:S(2)}, u32[]{:S(2)}) collective-permute-start(bf16[384,256]{1,0:T(8,128)(2,1)S(1)} %collective-permute-done.12.rm), channel_id=1, source_target_pairs={{0,1},{1,0},{2,3},{3,2},{4,5},{5,4},{6,7},{7,6},{8,9},{9,8},{10,11... | collective-permute-start | bytes 589832 | tf_op jit(solution)/shard_map/ppermute | solution.py:36
  120.9 1.1 copy-start.12
  120.9 2.3 %collective-permute-start.17 = (bf16[256,384]{1,0:T(8,128)(2,1)S(1)}, bf16[256,384]{1,0:T(8,128)(2,1)S(1)}, u32[]{:S(2)}, u32[]{:S(2)}) collective-permute-start(bf16[256,384]{1,0:T(8,128)(2,1)S(1)} %collective-permute-done.13.bm), channel_id=1, source_target_pairs={{0,1},{1,0},{2,3},{3,2},{4,5},{5,4},{6,7},{7,6},{8,9},{9,8},{10,11... | collective-permute-start | bytes 589832 | tf_op jit(solution)/shard_map/ppermute | solution.py:36
  137.7 2.1 %collective-permute-start.26 = (bf16[2,2,256,256]{3,2,1,0:T(8,128)(2,1)}, bf16[2,2,256,256]{3,2,1,0:T(8,128)(2,1)S(1)}, u32[]{:S(2)}, u32[]{:S(2)}) collective-permute-start(bf16[2,2,256,256]{3,2,1,0:T(8,128)(2,1)} %get-tuple-element.45), channel_id=1, source_target_pairs={{0,1},{1,0},{2,3},{3,2},{4,5},{5,4},{6,7},{7,6},{8,9},{9,8},{10,11... | collective-permute-start | bytes 1572872 | tf_op jit(solution)/shard_map/ppermute | solution.py:36
  137.7 7.9 %collective-permute-start.21 = (bf16[640,640]{1,0:T(8,128)(2,1)}, bf16[640,640]{1,0:T(8,128)(2,1)S(1)}, u32[]{:S(2)}, u32[]{:S(2)}) collective-permute-start(bf16[640,640]{1,0:T(8,128)(2,1)} %get-tuple-element.38), channel_id=1, source_target_pairs={{0,1},{1,0},{2,3},{3,2},{4,5},{5,4},{6,7},{7,6},{8,9},{9,8},{10,11... | collective-permute-start | bytes 2457608 | tf_op jit(solution)/shard_map/ppermute | solution.py:36
  141.9 33.9 %all-to-all-start.2 = ((bf16[16,64,256]{2,1,0:T(8,128)(2,1)}), bf16[16,64,256]{2,1,0:T(8,128)(2,1)S(1)}, u32[]{:S(2)}, u32[]{:S(2)}) async-start(bf16[16,64,256]{2,1,0:T(8,128)(2,1)} %bitcast.8), calls=%async_computation.2 | async-start | bytes 1048576 | tf_op jit(solution)/shard_map/all_to_all | solution.py:255
  149.1 16.7 %collective-permute-start.22 = (bf16[384,256]{1,0:T(8,128)(2,1)}, bf16[384,256]{1,0:T(8,128)(2,1)S(1)}, u32[]{:S(2)}, u32[]{:S(2)}) collective-permute-start(bf16[384,256]{1,0:T(8,128)(2,1)} %get-tuple-element.40), channel_id=1, source_target_pairs={{0,2},{2,4},{4,6},{6,8},{8,10},{10,12},{12,14},{14,16},{16,18},{18... | collective-permute-start | bytes 589832 | tf_op jit(solution)/shard_map/ppermute | solution.py:27
  150.9 21.6 %collective-permute-start.23 = (bf16[256,384]{1,0:T(8,128)(2,1)}, bf16[256,384]{1,0:T(8,128)(2,1)S(1)}, u32[]{:S(2)}, u32[]{:S(2)}) collective-permute-start(bf16[256,384]{1,0:T(8,128)(2,1)} %get-tuple-element.41), channel_id=1, source_target_pairs={{0,16},{2,18},{4,20},{6,22},{8,24},{10,26},{12,28},{14,30},{16,0},... | collective-permute-start | bytes 589832 | tf_op jit(solution)/shard_map/ppermute | solution.py:27
  153.3 12.5 %collective-permute-start.24 = (bf16[256,256]{1,0:T(8,128)(2,1)}, bf16[256,256]{1,0:T(8,128)(2,1)S(1)}, u32[]{:S(2)}, u32[]{:S(2)}) collective-permute-start(bf16[256,256]{1,0:T(8,128)(2,1)} %get-tuple-element.42), channel_id=1, source_target_pairs={{0,18},{2,20},{4,22},{6,24},{8,26},{10,28},{12,30},{14,0},{16,2},{... | collective-permute-start | bytes 393224 | tf_op jit(solution)/shard_map/ppermute | solution.py:27
  165.8 6.7 %copy-start.26 = (bf16[256,256]{1,0:T(8,128)(2,1)}, bf16[256,256]{1,0:T(8,128)(2,1)S(1)}, u32[]{:S(2)}) copy-start(bf16[256,256]{1,0:T(8,128)(2,1)S(1)} %collective-permute-done.24.diag) | copy-start | bytes 393220
  165.8 6.7 %copy-start.19 = (bf16[384,256]{1,0:T(8,128)(2,1)}, bf16[384,256]{1,0:T(8,128)(2,1)S(1)}, u32[]{:S(2)}) copy-start(bf16[384,256]{1,0:T(8,128)(2,1)S(1)} %collective-permute-done.22.right) | copy-start | bytes 589828
  175.8 9.7 %copy-start.7 = (f32[384,384]{1,0:T(8,128)S(1)}, f32[384,384]{1,0:T(8,128)}, u32[]{:S(2)}) copy-start(f32[384,384]{1,0:T(8,128)} %get-tuple-element.43) | copy-start | bytes 1769476
  175.8 9.7 %collective-permute-start.25 = (f32[384,384]{1,0:T(8,128)}, f32[384,384]{1,0:T(8,128)S(1)}, u32[]{:S(2)}, u32[]{:S(2)}) collective-permute-start(f32[384,384]{1,0:T(8,128)} %get-tuple-element.43), channel_id=1, source_target_pairs={{0,1},{1,0},{2,3},{3,2},{4,5},{5,4},{6,7},{7,6},{8,9},{9,8},{10,11... | collective-permute-start | bytes 1769480 | tf_op jit(solution)/shard_map/ppermute | solution.py:36
  176.8 24.3 %all-to-all-start.3 = ((bf16[16,64,256]{2,1,0:T(8,128)(2,1)}), bf16[16,64,256]{2,1,0:T(8,128)(2,1)S(1)}, u32[]{:S(2)}, u32[]{:S(2)}) async-start(bf16[16,64,256]{2,1,0:T(8,128)(2,1)} %broadcast_in_dim.8), calls=%async_computation.3 | async-start | bytes 1048576 | tf_op jit(solution)/shard_map/all_to_all | solution.py:258
  186.7 14.4 %copy-start = (f32[2,2,256,256]{3,2,1,0:T(8,128)S(1)}, f32[2,2,256,256]{3,2,1,0:T(8,128)}, u32[]{:S(2)}) copy-start(f32[2,2,256,256]{3,2,1,0:T(8,128)} %multiply_subtract_fusion.1.pm) | copy-start | bytes 3145732
  (13 other events, 9.9 us)
